TPU v7x, 32 devices: a whole 2x2x4 slice. The times are simulated.
32 devices in a mesh: groups: 2 (over y), ctx: 8 (over z, x), head: 2 (over core).
Axes of the slice: x: 2, y: 2, z: 4, core: 2. Of those that a mesh axis runs over, the one named last changes fastest.
Arguments:
- queries: bfloat16 [2048, 2048], P(('groups', 'ctx'), 'head'), parts along dimension 0, may hold values from -16 to 16
- key_states: bfloat16 [2048, 1024], P(('groups', 'ctx'), 'head'), parts along dimension 0, may hold values from -16 to 16
- value_states: bfloat16 [2048, 1024], P(('groups', 'ctx'), 'head'), parts along dimension 0, may hold values from -6 to 6
- out_grad: bfloat16 [2048, 2048], P(('groups', 'ctx'), 'head'), parts along dimension 0, may hold values from -6 to 6
- doc_ids: int32 [32], P('groups'), parts along dimension 0, may hold values from 0 to 5, never falling along the last dimension, each value on 1 to 8 neighbouring positions
- int_pos: int32 [128], P('groups'), parts along dimension 0, may hold values from 0 to 127, as said below
- hidden: bfloat16 [128, 4608], P('groups', 'ctx'), parts along dimension 0, may hold values from -6 to 6
- upstream: bfloat16 [128, 4608], P('groups', 'ctx'), parts along dimension 0, may hold values from -3 to 3
- w_query: bfloat16 [4608, 2048], P('ctx', 'head'), may hold values from -0.09375 to 0.09375
- w_key: bfloat16 [4608, 1024], P('ctx', 'head'), may hold values from -0.09375 to 0.09375
- w_value: bfloat16 [4608, 1024], P('ctx', 'head'), may hold values from -0.09375 to 0.09375
- rotation: float32 [8, 4608], P(None, 'ctx'), may hold values from -0.09375 to 0.09375
- projection: float32 [8, 4608], P(None, 'ctx'), may hold values from -0.09375 to 0.09375
- rank_bias: float32 [8], replicated, may hold values from -4 to 4
Outputs:
- grad_rot: float32 [16, 4608], P('groups', 'ctx'), parts along dimension 0
- grad_proj: float32 [16, 4608], P('groups', 'ctx'), parts along dimension 0
- grad_bias: float32 [16], P('groups'), parts along dimension 0
There are 2 independent parts, one for each index of `groups`. A program takes and returns all parts, laid end to end along the dimension named above; an argument that names none is the same for every part. Nothing has to cross between parts.
Inputs may be any that keep to these rules, and one draw needn't show every extreme that they name: `doc_ids`: ids never fall along the blocks; each document covers 1 to 8 consecutive blocks, and one covers exactly 8. `int_pos`: each aligned group of 8 entries belongs to one block of 128 tokens and holds distinct token indices inside that block in rising order.
All inputs are finite; a program needn't handle non-finite values.
Results may differ from a plain program's by a relative error of at most 0.004.
The roundings to bfloat16 on the way count: a program that leaves them out, or rounds other values in their place, can miss the bound.
Values may be sent and summed in bfloat16 or wider, within the bound.
A program may use at most 64 MiB of HBM per device.

v0:
```python
import jax
import jax.numpy as jnp
from jax import lax
from jax.sharding import PartitionSpec as P

HD = 128
BLK = 64
POS_DEV = 8
scale_q = 1.0 / 12.0
soft_cap = 50.0
key_block = 512


def capping(dot_vals):
    return soft_cap * jnp.tanh(dot_vals * scale_q / soft_cap)


def doc_lookup(doc_table, block_idx):
    table_ids = jnp.arange(doc_table.shape[0], dtype=jnp.int32)
    return jnp.sum(
        jnp.where(block_idx[:, None] == table_ids[None, :], doc_table[None, :], 0), axis=1
    )


def local(
    queries,
    key_states,
    value_states,
    out_grad,
    doc_ids,
    int_pos,
    hidden,
    upstream,
    w_query,
    w_key,
    w_value,
    rotation,
    projection,
    rank_bias,
):
    tokens = queries.shape[0]
    kv_width = key_states.shape[1]
    groups_kv = kv_width // HD
    per_group = queries.shape[1] // kv_width
    pick_count = POS_DEV
    ctx_index = lax.axis_index("ctx")
    my_pos = lax.dynamic_slice_in_dim(int_pos, ctx_index * pick_count, pick_count, 0)
    query_pos = ctx_index * tokens + jnp.arange(tokens, dtype=jnp.int32)
    query_doc = doc_lookup(doc_ids, query_pos // BLK)
    pick_pos = ctx_index * tokens + my_pos
    pick_doc = doc_lookup(doc_ids, pick_pos // BLK)
    query_heads = queries.reshape(tokens, groups_kv, per_group, HD)
    grad_heads = out_grad.reshape(tokens, groups_kv, per_group, HD)
    pick_query = jnp.take(queries, my_pos, axis=0).reshape(pick_count, groups_kv, per_group, HD)
    pick_grad = jnp.take(out_grad, my_pos, axis=0).reshape(pick_count, groups_kv, per_group, HD)

    def visit_keys(running, kv_rows, first_row):
        z_total, numerator, main_sum, side_sum = running
        row_count = kv_rows.shape[0]
        key_pos = first_row + jnp.arange(row_count, dtype=jnp.int32)
        key_doc = doc_lookup(doc_ids, key_pos // BLK)
        key_heads = kv_rows[:, :kv_width].reshape(row_count, groups_kv, HD)
        value_heads = kv_rows[:, kv_width:].reshape(row_count, groups_kv, HD)
        capped = capping(
            jnp.einsum("tgqd,rgd->gqtr", query_heads, key_heads, preferred_element_type=jnp.float32)
        )
        visible = (
            (key_pos[None, :] <= query_pos[:, None])
            & (key_doc[None, :] == query_doc[:, None])
            & (key_pos[None, :] >= 0)
        )
        weights = jnp.where(visible, jnp.exp(capped), 0.0)
        z_total = z_total + jnp.sum(weights, axis=-1)
        numerator = numerator + jnp.einsum(
            "gqtr,rgd->tgqd",
            weights.astype(jnp.bfloat16),
            value_heads,
            preferred_element_type=jnp.float32,
        )
        pick_capped = capping(
            jnp.einsum("pgqd,rgd->gqpr", pick_query, key_heads, preferred_element_type=jnp.float32)
        )
        pick_visible = (
            (key_pos[None, :] <= pick_pos[:, None])
            & (key_doc[None, :] == pick_doc[:, None])
            & (key_pos[None, :] >= 0)
        )
        pick_weights = jnp.where(
            pick_visible, jnp.exp(pick_capped) * (1.0 - (pick_capped / soft_cap) ** 2), 0.0
        )
        prob_grad = jnp.einsum(
            "pgqd,rgd->gqpr", pick_grad, value_heads, preferred_element_type=jnp.float32
        )
        main_sum = main_sum + jnp.einsum(
            "gqpr,rgd->pgqd",
            (pick_weights * prob_grad).astype(jnp.bfloat16),
            key_heads,
            preferred_element_type=jnp.float32,
        )
        side_sum = side_sum + jnp.einsum(
            "gqpr,rgd->pgqd",
            pick_weights.astype(jnp.bfloat16),
            key_heads,
            preferred_element_type=jnp.float32,
        )
        return (z_total, numerator, main_sum, side_sum)

    kv_local = jnp.concatenate([key_states, value_states], axis=1)
    start_state = (
        jnp.zeros((groups_kv, per_group, tokens), jnp.float32),
        jnp.zeros((tokens, groups_kv, per_group, HD), jnp.float32),
        jnp.zeros((pick_count, groups_kv, per_group, HD), jnp.float32),
        jnp.zeros((pick_count, groups_kv, per_group, HD), jnp.float32),
    )
    running = start_state
    kv_piece = lax.all_gather(kv_local, "ctx", axis=0, tiled=True)
    row_count = kv_piece.shape[0]

    def one_block(accum_state, block_no):
        block_rows = lax.dynamic_slice_in_dim(kv_piece, block_no * key_block, key_block, 0)
        return (visit_keys(accum_state, block_rows, block_no * key_block), None)

    running, _ = lax.scan(one_block, running, jnp.arange(row_count // key_block, dtype=jnp.int32))
    z_total, numerator, main_sum, side_sum = running
    z_tok = jnp.transpose(z_total, (2, 0, 1))
    outputs = numerator / z_tok[..., None]
    row_delta = jnp.sum(grad_heads.astype(jnp.float32) * outputs, axis=-1)
    pick_z = jnp.take(z_tok, my_pos, axis=0)
    pick_delta = jnp.take(row_delta, my_pos, axis=0)
    dq_rows = (
        (scale_q * (main_sum - pick_delta[..., None] * side_sum) / pick_z[..., None])
        .reshape(pick_count, queries.shape[1])
        .astype(jnp.bfloat16)
    )
    delta_heads = jnp.transpose(row_delta, (1, 2, 0))
    picked = jnp.concatenate(
        [jnp.take(key_states, my_pos, axis=0), jnp.take(value_states, my_pos, axis=0)], axis=1
    )
    gathered = lax.all_gather(picked, "ctx", axis=0, tiled=True)
    block_rows = gathered
    row_ids = jnp.arange(pick_count * lax.axis_size("ctx"), dtype=jnp.int32)
    key_pos = row_ids // pick_count * tokens + int_pos
    row_count = block_rows.shape[0]
    key_doc = doc_lookup(doc_ids, key_pos // BLK)
    key_heads = block_rows[:, :kv_width].reshape(row_count, groups_kv, HD)
    value_heads = block_rows[:, kv_width:].reshape(row_count, groups_kv, HD)
    capped = capping(
        jnp.einsum("tgqd,rgd->gqtr", query_heads, key_heads, preferred_element_type=jnp.float32)
    )
    visible = (key_pos[None, :] <= query_pos[:, None]) & (key_doc[None, :] == query_doc[:, None])
    probs = jnp.where(visible, jnp.exp(capped), 0.0) / z_total[..., None]
    prob_grad = jnp.einsum(
        "tgqd,rgd->gqtr", grad_heads, value_heads, preferred_element_type=jnp.float32
    )
    dscore = probs * (prob_grad - delta_heads[..., None]) * (1.0 - (capped / soft_cap) ** 2)
    value_grad = jnp.einsum(
        "gqtr,tgqd->rgd", probs.astype(jnp.bfloat16), grad_heads, preferred_element_type=jnp.float32
    )
    key_grad = scale_q * jnp.einsum(
        "gqtr,tgqd->rgd",
        dscore.astype(jnp.bfloat16),
        query_heads,
        preferred_element_type=jnp.float32,
    )
    key_sums = lax.psum_scatter(
        jnp.concatenate(
            [key_grad.reshape(row_count, kv_width), value_grad.reshape(row_count, kv_width)], axis=1
        ),
        "ctx",
        scatter_dimension=0,
        tiled=True,
    )
    pos_rows = jnp.concatenate([dq_rows, key_sums.astype(jnp.bfloat16)], axis=1)
    weight_cat = jnp.concatenate([w_query, w_key, w_value], axis=1)
    partial_grad = lax.dot_general(
        lax.all_gather(pos_rows, "ctx", axis=0, tiled=True),
        weight_cat,
        (((1,), (1,)), ((), ())),
        preferred_element_type=jnp.float32,
    )
    resid_grad = lax.psum(partial_grad, "head") + upstream.astype(jnp.float32)
    hidden_wide = hidden.astype(jnp.float32)
    rank_part = jnp.dot(resid_grad, rotation.T, precision=lax.Precision.HIGHEST)
    state_part = jnp.dot(hidden_wide, (projection - rotation).T, precision=lax.Precision.HIGHEST)
    rank_grad, rank_state = lax.psum((rank_part, state_part), "ctx")
    rank_state = rank_state + rank_bias[None, :]
    grad_bias = jnp.sum(rank_grad, axis=0)
    grad_proj = jnp.dot(rank_grad.T, hidden_wide, precision=lax.Precision.HIGHEST)
    grad_rot = jnp.dot(rank_state.T, resid_grad, precision=lax.Precision.HIGHEST) - grad_proj
    return (grad_rot, grad_proj, grad_bias)


def solution(mesh):
    in_specs = (
        P(("groups", "ctx"), "head"),
        P(("groups", "ctx"), "head"),
        P(("groups", "ctx"), "head"),
        P(("groups", "ctx"), "head"),
        P("groups"),
        P("groups"),
        P("groups", "ctx"),
        P("groups", "ctx"),
        P("ctx", "head"),
        P("ctx", "head"),
        P("ctx", "head"),
        P(None, "ctx"),
        P(None, "ctx"),
        P(),
    )
    out_specs = (P("groups", "ctx"), P("groups", "ctx"), P("groups"))
    return jax.shard_map(local, mesh=mesh, in_specs=in_specs, out_specs=out_specs, check_vma=False)
```

profile of v0, /device:TPU:0, one launch (start us, length us, event | category | flops | bytes accessed | tf_op | source)
XLA Modules:
  0.0 219.9 jit_solution(13700051381468569167)
XLA Ops:
  7.3 1.1 copy.98
  8.4 1.0 copy.99
  9.4 0.7 pad_maximum_fusion
  10.3 1.1 copy.100
  11.4 0.7 compare_and_fusion.1
  12.1 1.6 gather_fusion
  13.7 0.6 gather_fusion.1
  14.3 0.2 copy.102
  14.5 0.6 gather_fusion.4
  15.1 0.6 gather_fusion.5
  15.6 0.2 copy.101
  15.9 32.5 %all_gather.10 = bf16[64,1024]{1,0:T(8,128)(2,1)S(1)} all-gather(bf16[8,1024]{1,0:T(8,128)(2,1)S(1)} %pad_maximum_fusion.3), channel_id=1, replica_groups=mesh['groups'=2,'ctx'=8,'head'=2] {'ctx'}, dimensions={0}, use_global_device_ids=true | all-gather | bytes 147456 | tf_op jit(solution)/shard_map/all_gather | solution.py:139
  48.5 0.1 and_select_fusion.2
  48.6 0.2 select_reduce_fusion.3
  48.8 0.1 select_reduce_fusion.2
  48.9 0.1 select_reduce_fusion.1
  49.0 0.1 compare_and_fusion
  49.1 0.1 broadcast_select_fusion
  49.2 0.2 fusion.22
  49.4 15.3 %all-gather.2.cloned.1.call-done = bf16[1024,1024]{0,1:T(8,128)(2,1)} async-done(((bf16[128,1024]{0,1:T(8,128)(2,1)}), bf16[1024,1024]{0,1:T(8,128)(2,1)}) %all-gather.2.cloned.1.call-update) | async-done | bytes 2097168 | tf_op jit(solution)/shard_map/all_gather | solution.py:116
  64.7 10.2 %while.20 = (s32[]{:T(128)}, f32[4,2,128]{2,1,0:T(2,128)S(1)}, f32[128,4,2,128]{0,3,2,1:T(8,128)S(1)}, f32[8,4,2,128]{3,0,2,1:T(8,128)S(1)}, f32[8,4,2,128]{3,0,...) while((s32[]{:T(128)}, f32[4,2,128]{2,1,0:T(2,128)S(1)}, ...), condition=%wide.region_6.8_spmd.clone, body=%wide.region_3.7_spmd.clone.sunk | while | flops 305514112 | bytes 9383324 | solution.py:123
  64.7 0.6 dynamic_slice.26
  65.9 0.1 select_reduce_fusion.5
  66.0 0.1 and_and_fusion.5
  66.1 1.3 fusion.113
  67.4 0.2 bitcast_select_fusion.4
  67.6 0.3 fusion.117
  67.9 0.3 and_and_fusion.4
  68.2 0.9 fusion.115
  69.1 0.4 fusion.116
  69.5 0.2 fusion.118
  69.8 0.6 dynamic_slice.26
  71.0 0.1 select_reduce_fusion.5
  71.1 0.1 and_and_fusion.5
  71.2 1.3 fusion.113
  72.5 0.2 bitcast_select_fusion.4
  72.7 0.3 fusion.117
  73.0 0.3 and_and_fusion.4
  73.3 0.9 fusion.115
  74.2 0.4 fusion.116
  74.6 0.2 fusion.118
  74.9 0.1 multiply_reduce_fusion
  75.0 0.2 convolution_bitcast_fusion.4
  75.2 0.3 fusion.28
  75.6 0.7 pad_maximum_fusion.1
  76.3 0.2 copy.105
  76.5 0.2 copy.103
  76.7 0.6 gather_fusion.2
  77.2 0.6 gather_fusion.3
  77.8 0.1 broadcast_select_fusion.3
  77.9 0.1 copy.106
  78.0 0.1 copy.107
  78.1 0.1 divide_convert_fusion
  78.2 57.9 %reduce-scatter.2.cloned.1.call-done = f32[8,1024]{1,0:T(8,128)} async-done(((f32[64,1024]{1,0:T(8,128)}), f32[8,1024]{1,0:T(8,128)}) %reduce-scatter.2.cloned.1.call-update) | async-done | bytes 32784 | tf_op jit(solution)/shard_map/reduce_scatter | solution.py:165
  136.1 0.8 convert_element_type.48
  136.8 30.9 %all_gather.11 = bf16[64,2048]{1,0:T(8,128)(2,1)S(1)} all-gather(bf16[8,2048]{1,0:T(8,128)(2,1)S(1)} %pad_maximum_fusion.2), channel_id=1, replica_groups=mesh['groups'=2,'ctx'=8,'head'=2] {'ctx'}, dimensions={0}, use_global_device_ids=true | all-gather | bytes 294912 | tf_op jit(solution)/shard_map/all_gather | solution.py:176
  167.8 2.8 %fusion.16 = f32[64,576]{1,0:T(8,128)} fusion(bf16[64,2048]{1,0:T(8,128)(2,1)S(1)} %all_gather.11, bf16[576,512]{1,0:T(8,128)(2,1)} %param.32, bf16[576,512]{1,0:T(8,128)(2,1)} %param.31, bf16[576,1024]{1,0:T(8,128)(2,1)S(1)} %copy-done.11), kind=kOutput, calls=%fused_computation.40 | convolution fusion | flops 158072832 | bytes 2768896 | tf_op jit(solution)/shard_map/dot_general | solution.py:175
  170.6 0.1 convolution_bitcast_fusion.6
  170.7 17.0 %all-reduce.3.cloned.1.call-done = f32[64,576]{1,0:T(8,128)} async-done(((f32[64,576]{1,0:T(8,128)}), f32[64,576]{1,0:T(8,128)}) %all-reduce.3.cloned.1.call-update) | async-done | bytes 147472 | tf_op jit(solution)/shard_map/psum | solution.py:181
  187.8 1.1 fusion.46
  188.9 21.9 %all-reduce = (f32[64,8]{0,1:T(8,128)S(1)}, f32[64,8]{0,1:T(8,128)S(1)}) all-reduce(f32[64,8]{0,1:T(8,128)S(1)} %fusion.46, f32[64,8]{0,1:T(8,128)S(1)} %convolution_bitcast_fusion.6), channel_id=1, replica_groups=mesh['groups'=2,'ctx'=8,'head'=2] {'ctx'}, use_global_device_ids=true, to_apply=%region_11.15 | all-reduce | flops 1024 | bytes 8192 | tf_op jit(solution)/shard_map/psum | solution.py:185
  210.8 0.1 fusion.65
  211.0 0.6 reduce_sum.75
  211.6 1.8 convolution_subtract_fusion
  (54 shorter events, 0.5 us)
Async XLA Ops:
  7.2 163.4 %copy-start = (bf16[64,576]{1,0:T(8,128)(2,1)S(1)}, bf16[64,576]{1,0:T(8,128)(2,1)}, u32[]{:S(2)}) copy-start(bf16[64,576]{1,0:T(8,128)(2,1)} %param.28) | copy-start | bytes 221188
  7.2 7.3 %copy-start.3 = (bf16[128,512]{1,0:T(8,128)(2,1)S(1)}, bf16[128,512]{1,0:T(8,128)(2,1)}, u32[]{:S(2)}) copy-start(bf16[128,512]{1,0:T(8,128)(2,1)} %param.23) | copy-start | bytes 393220
  7.2 7.9 %copy-start.4 = (bf16[128,512]{1,0:T(8,128)(2,1)S(1)}, bf16[128,512]{1,0:T(8,128)(2,1)}, u32[]{:S(2)}) copy-start(bf16[128,512]{1,0:T(8,128)(2,1)} %param.24) | copy-start | bytes 393220
  7.2 41.3 %copy-start.9 = (s32[64]{0:T(128)S(1)}, s32[64]{0:T(128)}, u32[]{:S(2)}) copy-start(s32[64]{0:T(128)} %param.27) | copy-start | bytes 772
  7.2 6.5 %copy-start.1 = (bf16[128,1024]{1,0:T(8,128)(2,1)S(1)}, bf16[128,1024]{1,0:T(8,128)(2,1)}, u32[]{:S(2)}) copy-start(bf16[128,1024]{1,0:T(8,128)(2,1)} %param.25) | copy-start | bytes 786436
  7.2 41.4 %copy-start.8 = (s32[16]{0:T(128)S(1)}, s32[16]{0:T(128)}, u32[]{:S(2)}) copy-start(s32[16]{0:T(128)} %param.26) | copy-start | bytes 196
  7.2 57.4 %all-gather.2.cloned.1.call-start = ((), (), s32[]{:S(2)}) async-start(), calls=%async_computation.1 | async-start | bytes 2359296 | tf_op jit(solution)/shard_map/all_gather | solution.py:116
  10.2 125.9 %reduce-scatter.2.cloned.1.call-start = ((), (), s32[]{:S(2)}) async-start(), calls=%async_computation.2 | async-start | bytes 294912 | tf_op jit(solution)/shard_map/reduce_scatter | solution.py:165
  75.2 92.6 %copy-start.11 = (bf16[576,1024]{1,0:T(8,128)(2,1)S(1)}, bf16[576,1024]{1,0:T(8,128)(2,1)}, u32[]{:S(2)}) copy-start(bf16[576,1024]{1,0:T(8,128)(2,1)} %param.30) | copy-start | bytes 3538948
  76.3 111.5 %all-reduce.3.cloned.1.call-start = ((), (), s32[]{:S(2)}) async-start(), calls=%async_computation.3 | async-start | bytes 327680 | tf_op jit(solution)/shard_map/psum | solution.py:181
  167.8 2.8 %copy-start.5 = (f32[8,576]{1,0:T(8,128)S(1)}, f32[8,576]{1,0:T(8,128)}, u32[]{:S(2)}) copy-start(f32[8,576]{1,0:T(8,128)} %param.33) | copy-start | bytes 55300
  167.8 2.9 %copy-start.7 = (f32[8,576]{1,0:T(8,128)S(1)}, f32[8,576]{1,0:T(8,128)}, u32[]{:S(2)}) copy-start(f32[8,576]{1,0:T(8,128)} %param.34) | copy-start | bytes 55300
  167.8 20.0 %copy-start.2 = (bf16[64,576]{1,0:T(8,128)(2,1)S(1)}, bf16[64,576]{1,0:T(8,128)(2,1)}, u32[]{:S(2)}) copy-start(bf16[64,576]{1,0:T(8,128)(2,1)} %param.29) | copy-start | bytes 221188
  167.8 43.8 %copy-start.10 = (f32[8]{0:T(128)S(1)}, f32[8]{0:T(128)}, u32[]{:S(2)}) copy-start(f32[8]{0:T(128)} %param.35) | copy-start | bytes 100
  211.0 2.4 %copy-start.6 = (f32[8,576]{1,0:T(8,128)}, f32[8,576]{1,0:T(8,128)S(1)}, u32[]{:S(2)}) copy-start(f32[8,576]{1,0:T(8,128)S(1)} %fusion.65) | copy-start | bytes 55300
Sparse Core Ops, SparseCore 0:
  10.3 54.3 all-gather.1
  76.4 59.6 reduce-scatter.1
  170.7 17.0 all-reduce.2
where the time goes:
time: 220 us
  waiting for transfers between devices  90.3 us (41%)
  blocking collectives  85.3 us (39%)
  between operations  14.1 us (6%)
  local copies, waits for them, and re-layouts  12.4 us (6%)
  matrix products  10.7 us (5%)
  other arithmetic  5.58 us (3%)
    reduce_scatter x1, waiting for transfers between devices, local(): lax.psum_scatter(jnp.concatenate([key_grad.reshape(row_count, kv_width),...  57.9 us
    all_gather x1, blocking collectives, local(): gathered = lax.all_gather(picked, 'ctx', axis=0, tiled=True)  32.5 us
    all_gather x1, blocking collectives, local(): lax.all_gather(pos_rows, 'ctx', axis=0, tiled=True)  30.9 us
    psum x1, blocking collectives, local(): rank_grad, rank_state = lax.psum((rank_part, state_part), 'ctx')  21.9 us
    psum x1, waiting for transfers between devices, local(): resid_grad = lax.psum(partial_grad, 'head') + upstream.astype(jnp.float32)  17 us
    all_gather x1, waiting for transfers between devices, local(): kv_piece = lax.all_gather(kv_local, 'ctx', axis=0, tiled=True)  15.3 us
  transfers between devices with their start and end apart: 3, of which 3 were waited for; matrix products, arithmetic and copies ran while one was open for 4% of the time, Pallas kernels for 0%

commit v1 on v0

--- a/solution.py
+++ b/solution.py
@@ -9,6 +9,24 @@
 scale_q = 1.0 / 12.0
 soft_cap = 50.0
 key_block = 512
+
+
+def joined_along(pieces, dim):
+    pieces = jnp.moveaxis(pieces, 0, dim)
+    lengths = pieces.shape
+    return pieces.reshape(*lengths[:dim], lengths[dim] * lengths[dim + 1], *lengths[dim + 2 :])
+
+
+def collected_by_bits(x, axis):
+    size = lax.axis_size(axis)
+    blocks = x[None]
+    for level in range(size.bit_length() - 1):
+        bit = 1 << level
+        theirs = lax.ppermute(blocks, axis, [(i, i ^ bit) for i in range(size)])
+        both = jnp.stack([blocks, theirs])
+        upper = lax.axis_index(axis) >> level & 1
+        blocks = jnp.where(upper == 0, both, both[::-1]).reshape(-1, *x.shape)
+    return blocks
 
 
 def capping(dot_vals):
@@ -113,7 +131,7 @@
         jnp.zeros((pick_count, groups_kv, per_group, HD), jnp.float32),
     )
     running = start_state
-    kv_piece = lax.all_gather(kv_local, "ctx", axis=0, tiled=True)
+    kv_piece = joined_along(collected_by_bits(kv_local, "ctx"), 0)
     row_count = kv_piece.shape[0]
 
     def one_block(accum_state, block_no):

time: 220 us -> 270 us (1.23)
  waiting for transfers between devices: 90.3 us -> 112 us
  other arithmetic: 5.58 us -> 14 us
  blocking collectives: 85.3 us -> 90.8 us
  starting transfers between devices: 0.12 us -> 5.05 us
  local copies, waits for them, and re-layouts: 12.4 us -> 17.3 us
  matrix products: 10.7 us -> 14.3 us
    ppermute x0 -> x3, waiting for transfers between devices: none -> 36 us  [collected_by_bits(): theirs = lax.ppermute(blocks, axis, [(i, i ^ bit) for i in range(size)])]
    all_gather x1 -> x0, waiting for transfers between devices: 15.3 us -> none  [local(): kv_piece = lax.all_gather(kv_local, 'ctx', axis=0, tiled=True)]
    all_gather x1, blocking collectives: 32.5 us -> 38.1 us  [local(): gathered = lax.all_gather(picked, 'ctx', axis=0, tiled=True)]
    ppermute x0 -> x3, starting transfers between devices: none -> 4.97 us  [collected_by_bits(): theirs = lax.ppermute(blocks, axis, [(i, i ^ bit) for i in range(size)])]
    another operation x0 -> x2, local copies, waits for them, and re-layouts: none -> 3.98 us  [the longest x1 3.23 us: joined_along(): pieces.reshape(*lengths[:dim], lengths[dim] * lengths[dim + 1], *lengths[...]
    another operation x0 -> x4, other arithmetic: none -> 3.02 us  [collected_by_bits(): both = jnp.stack([blocks, theirs])]
  transfers between devices with their start and end apart: 3 -> 5, of which waited for: 3 -> 4; matrix products, arithmetic and copies ran while one was open for 4% -> 5% of each run, Pallas kernels for 0% -> 0%
where the time goes in v1:
time: 270 us; the launch traced here: 269 us
  waiting for transfers between devices  112 us (41%)
  blocking collectives  90.8 us (34%)
  local copies, waits for them, and re-layouts  17.3 us (6%)
  between operations  14.5 us (5%)
  matrix products  14.3 us (5%)
  other arithmetic  14 us (5%)
  starting transfers between devices  5.05 us (2%)
    reduce_scatter x1, waiting for transfers between devices, local(): lax.psum_scatter(jnp.concatenate([key_grad.reshape(row_count, kv_width),...  58.6 us
    all_gather x1, blocking collectives, local(): gathered = lax.all_gather(picked, 'ctx', axis=0, tiled=True)  38.1 us
    ppermute x3, waiting for transfers between devices, collected_by_bits(): theirs = lax.ppermute(blocks, axis, [(i, i ^ bit) for i in range(size)])  36 us
    all_gather x1, blocking collectives, local(): lax.all_gather(pos_rows, 'ctx', axis=0, tiled=True)  30.9 us
    psum x1, blocking collectives, local(): rank_grad, rank_state = lax.psum((rank_part, state_part), 'ctx')  21.9 us
    psum x1, waiting for transfers between devices, local(): resid_grad = lax.psum(partial_grad, 'head') + upstream.astype(jnp.float32)  17.1 us
  transfers between devices with their start and end apart: 5, of which 4 were waited for; matrix products, arithmetic and copies ran while one was open for 5% of the time, Pallas kernels for 0%

profile of v1, /device:TPU:0, one launch (start us, length us, event | category | flops | bytes accessed | tf_op | source)
XLA Modules:
  0.0 269.3 jit_solution(13987661548030289032)
XLA Ops:
  7.2 0.9 constant_dynamic-update-slice_fusion.1
  8.2 0.9 constant_dynamic-update-slice_fusion
  9.1 3.0 %collective-permute-start = (bf16[1,128,1024]{2,1,0:T(8,128)(2,1)S(1)}, bf16[1,128,1024]{2,1,0:T(8,128)(2,1)S(1)}, u32[]{:S(2)}, u32[]{:S(2)}) collective-permute-start(bf16[1,128,1024]{2,1,0:T(8,128)(2,1)S(1)} %bitcast.189), channel_id=1, source_target_pairs={{0,2},{2,0},{4,6},{6,4},{8,10},{10,8},{12,14},{14,12},{1,3},{3,1},... | collective-permute-start | bytes 786440 | tf_op jit(solution)/shard_map/ppermute | solution.py:25
  12.1 0.7 compare_and_fusion.1
  12.8 1.5 gather_fusion.4
  14.3 1.5 gather_fusion.5
  15.9 2.5 collective-permute-done
  18.4 0.2 fusion.30
  18.6 1.9 collective-permute-start.1
  20.6 38.1 %all_gather.6 = bf16[64,1024]{1,0:T(8,128)(2,1)S(1)} all-gather(bf16[8,1024]{1,0:T(8,128)(2,1)S(1)} %pad_maximum_fusion.5), channel_id=1, replica_groups=mesh['groups'=2,'ctx'=8,'head'=2] {'ctx'}, dimensions={0}, use_global_device_ids=true | all-gather | bytes 147456 | tf_op jit(solution)/shard_map/all_gather | solution.py:157
  58.7 0.7 select_reduce_fusion.3
  59.5 0.3 reverse_select_fusion.1
  59.8 0.8 copy.98
  60.7 0.6 gather_fusion
  61.3 0.2 copy.100
  61.6 0.6 gather_fusion.1
  62.1 0.8 copy.102
  63.0 0.8 copy.101
  64.0 0.7 compare_and_fusion
  64.7 0.9 fusion.22
  65.6 0.7 copy.99
  66.4 33.5 %collective-permute-done.2 = bf16[4,128,1024]{1,0,2:T(4,128)(2,1)} collective-permute-done((bf16[4,128,1024]{1,0,2:T(4,128)(2,1)S(1)}, bf16[4,128,1024]{1,0,2:T(4,128)(2,1)}, u32[]{:S(2)}, u32[]{:S(2)}) %collective-permute-start.2) | collective-permute-done | bytes 1048608 | tf_op jit(solution)/shard_map/ppermute | solution.py:25
  99.9 2.7 %pad_maximum_fusion = bf16[2,4,128,1024]{2,1,0,3:T(4,128)(2,1)S(1)} fusion(bf16[1,4,128,1024]{2,1,0,3:T(4,128)(2,1)} %bitcast.9, bf16[1,4,128,1024]{2,1,0,3:T(4,128)(2,1)S(1)} %copy.99), kind=kLoop, calls=%fused_computation.47 | loop fusion | flops 1048576 | bytes 4194304 | tf_op jit(solution)/shard_map/stack | solution.py:26
  102.6 2.4 reverse_select_fusion
  105.0 3.2 %reshape_reshape.3 = bf16[1024,1024]{0,1:T(8,128)(2,1)S(1)} reshape(bf16[2,4,128,1024]{2,1,0,3:T(4,128)(2,1)} %reverse_select_fusion) | data formatting | bytes 4194304 | tf_op jit(solution)/shard_map/reshape;reshape | solution.py:17
  108.3 12.5 %while.20 = (s32[]{:T(128)}, f32[4,2,128]{2,1,0:T(2,128)S(1)}, f32[128,4,2,128]{0,3,2,1:T(8,128)}, f32[8,4,2,128]{3,0,2,1:T(8,128)S(1)}, f32[8,4,2,128]{3,0,2,1:...) while((s32[]{:T(128)}, f32[4,2,128]{2,1,0:T(2,128)S(1)}, ...), condition=%wide.region_6.8_spmd.clone, body=%wide.region_3.7_spmd.clone.sunk | while | flops 305514112 | bytes 13577804 | solution.py:141
  108.3 0.7 dynamic_slice.26
  109.8 0.7 and_and_fusion.5
  110.5 0.1 fusion.115
  110.6 0.2 bitcast_select_fusion.4
  110.8 0.3 fusion.119
  111.1 0.3 and_and_fusion.4
  111.4 1.9 fusion.117
  113.4 0.4 fusion.118
  113.7 0.2 fusion.120
  114.0 0.6 copy-done.2
  114.6 0.7 dynamic_slice.26
  116.1 0.7 and_and_fusion.5
  116.8 0.2 bitcast_select_fusion.4
  117.1 0.3 fusion.119
  117.4 0.3 and_and_fusion.4
  117.7 1.9 fusion.117
  119.6 0.4 fusion.118
  120.0 0.2 fusion.120
  120.2 0.6 copy-done.2
  120.9 1.3 multiply_reduce_fusion
  122.1 1.2 convolution_bitcast_fusion.4
  123.5 0.3 fusion.28
  123.8 0.7 pad_maximum_fusion.3
  124.6 0.2 copy.105
  124.8 0.2 copy.103
  124.9 0.7 gather_fusion.2
  125.6 0.7 gather_fusion.3
  126.7 58.6 %reduce-scatter.2.cloned.1.call-done = f32[8,1024]{1,0:T(8,128)} async-done(((f32[64,1024]{1,0:T(8,128)}), f32[8,1024]{1,0:T(8,128)}) %reduce-scatter.2.cloned.1.call-update) | async-done | bytes 32784 | tf_op jit(solution)/shard_map/reduce_scatter | solution.py:183
  185.3 0.8 convert_element_type.48
  186.1 30.9 %all_gather.7 = bf16[64,2048]{1,0:T(8,128)(2,1)S(1)} all-gather(bf16[8,2048]{1,0:T(8,128)(2,1)S(1)} %pad_maximum_fusion.4), channel_id=1, replica_groups=mesh['groups'=2,'ctx'=8,'head'=2] {'ctx'}, dimensions={0}, use_global_device_ids=true | all-gather | bytes 294912 | tf_op jit(solution)/shard_map/all_gather | solution.py:194
  217.0 2.6 fusion.16
  219.7 0.1 convolution_bitcast_fusion.6
  219.8 17.1 %all-reduce.3.cloned.1.call-done = f32[64,576]{1,0:T(8,128)} async-done(((f32[64,576]{1,0:T(8,128)}), f32[64,576]{1,0:T(8,128)}) %all-reduce.3.cloned.1.call-update) | async-done | bytes 147472 | tf_op jit(solution)/shard_map/psum | solution.py:199
  236.9 1.1 fusion.48
  238.0 21.9 %all-reduce = (f32[64,8]{0,1:T(8,128)S(1)}, f32[64,8]{0,1:T(8,128)S(1)}) all-reduce(f32[64,8]{0,1:T(8,128)S(1)} %fusion.48, f32[64,8]{0,1:T(8,128)S(1)} %convolution_bitcast_fusion.6), channel_id=1, replica_groups=mesh['groups'=2,'ctx'=8,'head'=2] {'ctx'}, use_global_device_ids=true, to_apply=%region_11.15 | all-reduce | flops 1024 | bytes 8192 | tf_op jit(solution)/shard_map/psum | solution.py:203
  259.9 0.1 fusion.67
  260.1 0.6 reduce_sum.75
  260.7 1.8 convolution_subtract_fusion
  (97 shorter events, 1.7 us)
Async XLA Ops:
  7.2 212.5 %copy-start = (bf16[64,576]{1,0:T(8,128)(2,1)S(1)}, bf16[64,576]{1,0:T(8,128)(2,1)}, u32[]{:S(2)}) copy-start(bf16[64,576]{1,0:T(8,128)(2,1)} %param.28) | copy-start | bytes 221188
  7.2 13.3 %copy-start.18 = (s32[64]{0:T(128)S(1)}, s32[64]{0:T(128)}, u32[]{:S(2)}) copy-start(s32[64]{0:T(128)} %param.27) | copy-start | bytes 772
  7.2 51.5 %copy-start.13 = (s32[16]{0:T(128)S(1)}, s32[16]{0:T(128)}, u32[]{:S(2)}) copy-start(s32[16]{0:T(128)} %param.26) | copy-start | bytes 196
  7.2 178.1 %reduce-scatter.2.cloned.1.call-start = ((), (), s32[]{:S(2)}) async-start(), calls=%async_computation.1 | async-start | bytes 294912 | tf_op jit(solution)/shard_map/reduce_scatter | solution.py:183
  9.1 9.3 %collective-permute-start = (bf16[1,128,1024]{2,1,0:T(8,128)(2,1)S(1)}, bf16[1,128,1024]{2,1,0:T(8,128)(2,1)S(1)}, u32[]{:S(2)}, u32[]{:S(2)}) collective-permute-start(bf16[1,128,1024]{2,1,0:T(8,128)(2,1)S(1)} %bitcast.189), channel_id=1, source_target_pairs={{0,2},{2,0},{4,6},{6,4},{8,10},{10,8},{12,14},{14,12},{1,3},{3,1},... | collective-permute-start | bytes 786440 | tf_op jit(solution)/shard_map/ppermute | solution.py:25
  12.8 51.8 %copy-start.15 = (pred[8]{0:T(512)(128)(4,1)}, pred[8]{0:T(512)(128)(4,1)S(1)}, u32[]{:S(2)}) copy-start(pred[8]{0:T(512)(128)(4,1)S(1)} %get-tuple-element.405) | copy-start | bytes 28
  12.8 48.7 %copy-start.14 = (s32[1024]{0:T(1024)}, s32[1024]{0:T(1024)S(1)}, u32[]{:S(2)}) copy-start(s32[1024]{0:T(1024)S(1)} %pad_clamp_fusion) | copy-start | bytes 12292
  18.6 40.8 %collective-permute-start.1 = (bf16[2,128,1024]{2,1,0:T(8,128)(2,1)S(1)}, bf16[2,128,1024]{2,1,0:T(8,128)(2,1)S(1)}, u32[]{:S(2)}, u32[]{:S(2)}) collective-permute-start(bf16[2,128,1024]{2,1,0:T(8,128)(2,1)S(1)} %get-tuple-element.414), channel_id=1, source_target_pairs={{0,4},{2,6},{4,0},{6,2},{8,12},{10,14},{12,8},{14,10},{1,5},{3,7},... | collective-permute-start | bytes 1572872 | tf_op jit(solution)/shard_map/ppermute | solution.py:25
  59.5 1.2 copy-start.6
  59.5 2.0 copy-start.7
  60.6 39.3 %collective-permute-start.2 = (bf16[4,128,1024]{1,0,2:T(4,128)(2,1)S(1)}, bf16[4,128,1024]{1,0,2:T(4,128)(2,1)}, u32[]{:S(2)}, u32[]{:S(2)}) collective-permute-start(bf16[4,128,1024]{1,0,2:T(4,128)(2,1)S(1)} %copy.98), channel_id=1, source_target_pairs={{0,8},{2,10},{4,12},{6,14},{8,0},{10,2},{12,4},{14,6},{1,9},{3,11}... | collective-permute-start | bytes 3145736 | tf_op jit(solution)/shard_map/ppermute | solution.py:25
  61.5 4.1 %copy-start.3 = (bf16[128,1024]{0,1:T(8,128)(2,1)}, bf16[128,1024]{0,1:T(8,128)(2,1)S(1)}, u32[]{:S(2)}) copy-start(bf16[128,1024]{0,1:T(8,128)(2,1)S(1)} %copy.100) | copy-start | bytes 786436
  108.3 1.5 copy-start.22
  111.4 1.9 copy-start.1
  113.3 1.2 copy-start.23
  113.7 0.8 copy-start.2
  114.6 1.5 copy-start.22
  117.7 1.9 copy-start.1
  119.6 1.2 copy-start.23
  120.0 0.8 copy-start.2
  120.8 2.6 copy-start.4
  120.9 2.6 copy-start.5
  120.9 2.6 copy-start.9
  120.9 2.6 copy-start.17
  123.4 2.9 %copy-start.16 = (pred[8]{0:T(512)(128)(4,1)S(1)}, pred[8]{0:T(512)(128)(4,1)}, u32[]{:S(2)}) copy-start(pred[8]{0:T(512)(128)(4,1)} %copy-done.15) | copy-start | bytes 28
  123.4 93.6 %copy-start.20 = (bf16[576,1024]{1,0:T(8,128)(2,1)S(1)}, bf16[576,1024]{1,0:T(8,128)(2,1)}, u32[]{:S(2)}) copy-start(bf16[576,1024]{1,0:T(8,128)(2,1)} %param.30) | copy-start | bytes 3538948
  123.4 93.5 %copy-start.21 = (bf16[576,512]{1,0:T(8,128)(2,1)S(1)}, bf16[576,512]{1,0:T(8,128)(2,1)}, u32[]{:S(2)}) copy-start(bf16[576,512]{1,0:T(8,128)(2,1)} %param.32) | copy-start | bytes 1769476
  124.6 112.3 %all-reduce.3.cloned.1.call-start = ((), (), s32[]{:S(2)}) async-start(), calls=%async_computation.2 | async-start | bytes 327680 | tf_op jit(solution)/shard_map/psum | solution.py:199
  217.0 2.7 copy-start.10
  217.0 2.7 copy-start.12
  217.0 19.9 %copy-start.8 = (bf16[64,576]{1,0:T(8,128)(2,1)S(1)}, bf16[64,576]{1,0:T(8,128)(2,1)}, u32[]{:S(2)}) copy-start(bf16[64,576]{1,0:T(8,128)(2,1)} %param.29) | copy-start | bytes 221188
  217.0 43.7 %copy-start.19 = (f32[8]{0:T(128)S(1)}, f32[8]{0:T(128)}, u32[]{:S(2)}) copy-start(f32[8]{0:T(128)} %param.35) | copy-start | bytes 100
  260.1 2.4 copy-start.11
Sparse Core Ops, SparseCore 0:
  124.7 60.5 reduce-scatter.1
  219.8 17.0 all-reduce.2
